TPU v7x, 512 devices: a whole 4x8x8 slice. The times are simulated.
512 devices in a mesh: row: 32 (over z_hi, y, core), col: 16 (over z_lo, x).
Axes of the slice: x: 4, y: 8, z: 8 (z_hi: 2, z_lo: 4; z = z_hi * 4 + z_lo), core: 2. Of those that a mesh axis runs over, the one named last changes fastest.
Arguments:
- mask_logits: float32 [4096, 2048], P('row', 'col'), may hold values from -6 to 6
- target: float32 [4096, 2048], P('row', 'col'), may hold values from 0 to 1
- weight: float32 [4096, 2048], P('row', 'col'), may hold values from 0.004 to 10, as said below
- kernels: float32 [2, 12288], P(None, ('row', 'col')), may hold values from -3 to 3
Outputs:
- new_logits: float32 [4096, 2048], P('row', 'col')
- loss_value: float32 [], replicated
Inputs may be any that keep to these rules, and one draw needn't show every extreme that they name: `weight`: positive loss weights.
All inputs are finite; a program needn't handle non-finite values.
Results may differ from a plain program's by a relative error of at most 0.0003.
Values sent between devices are 32-bit elements; how exact they have to be, the bound alone decides.
A program may use at most 64 MiB of HBM per device.

v0:
```python
import math
import jax
import jax.numpy as jnp
from jax import lax
from jax.sharding import PartitionSpec as P

HALO = 64
KERNELS = 6
BAND = 32
CONDITIONS = 2
SHARPNESS = 6.0
THRESHOLD = 0.75
STEP = 0.5
EPSILON = 1e-06
DOSES = (1.0, 1.15)


def padded_2(block, sides, width):
    for axis, dim in sides:
        count = lax.axis_size(axis)
        forward = [(i, i + 1) for i in range(count - 1)]
        backward = [(target, source) for source, target in forward]
        low = lax.ppermute(
            lax.slice_in_dim(block, block.shape[dim] - width, None, axis=dim), axis, forward
        )
        high = lax.ppermute(lax.slice_in_dim(block, 0, width, axis=dim), axis, backward)
        block = jnp.concatenate([low, block, high], axis=dim)
    return block


def matmul(first, second):
    return jnp.matmul(
        first, second, precision=lax.Precision.HIGHEST, preferred_element_type=jnp.float32
    )


def cmatmul(first_re, first_im, second_re, second_im):
    return (
        matmul(first_re, second_re) - matmul(first_im, second_im),
        matmul(first_re, second_im) + matmul(first_im, second_re),
    )


def dft_rows(band, pad_width):
    freq = jnp.arange(band, dtype=jnp.int32) - band // 2
    place = jnp.arange(pad_width, dtype=jnp.int32)
    turns = (freq[:, None] * place[None, :] % pad_width).astype(jnp.float32) * (
        2.0 * math.pi / pad_width
    )
    factor = 1.0 / math.sqrt(pad_width)
    return (jnp.cos(turns) * factor, -jnp.sin(turns) * factor)


def synthesize(spec_re, spec_im, wave_re, wave_im):
    left_re, left_im = cmatmul(wave_re.T, -wave_im.T, spec_re, spec_im)
    return cmatmul(left_re, left_im, wave_re, -wave_im)


def analyse(cell_re, cell_im, wave_re, wave_im):
    left_re, left_im = cmatmul(wave_re, wave_im, cell_re, cell_im)
    return cmatmul(left_re, left_im, wave_re.T, wave_im.T)


def tile_terms(padded_tile, kernel_re, kernel_im, wave_re, wave_im, dose, margin):
    mask_tile, target_tile, weight_tile = (padded_tile[0], padded_tile[1], padded_tile[2])
    pad_width = mask_tile.shape[0]
    core_width = pad_width - 2 * margin
    four_re, four_im = cmatmul(
        matmul(wave_re, mask_tile), matmul(wave_im, mask_tile), wave_re.T, wave_im.T
    )
    prod_re = four_re[None] * kernel_re - four_im[None] * kernel_im
    prod_im = four_re[None] * kernel_im + four_im[None] * kernel_re
    fields_re, fields_im = synthesize(prod_re, prod_im, wave_re, wave_im)
    intensity = jnp.sum(fields_re * fields_re + fields_im * fields_im, axis=0)
    resist = jax.nn.sigmoid(SHARPNESS * (dose * intensity - THRESHOLD))
    error_map = resist - target_tile
    inner = (weight_tile * error_map * error_map)[
        margin : margin + core_width, margin : margin + core_width
    ]
    tile_loss = jnp.sum(inner)
    slope_map = 2.0 * SHARPNESS * dose * weight_tile * error_map * resist * (1.0 - resist)
    back_re, back_im = analyse(
        slope_map[None] * fields_re, slope_map[None] * fields_im, wave_re, wave_im
    )
    sum_re = jnp.sum(kernel_re * back_re + kernel_im * back_im, axis=0)
    sum_im = jnp.sum(kernel_re * back_im - kernel_im * back_re, axis=0)
    core_re = wave_re[:, margin : margin + core_width]
    core_im = wave_im[:, margin : margin + core_width]
    left_re, left_im = cmatmul(core_re.T, -core_im.T, sum_re, sum_im)
    real_part = matmul(left_re, core_re) + matmul(left_im, core_im)
    return (2.0 * real_part, tile_loss)


def shards(mask_logits, target, weight, kernels):
    mask_cells = jax.nn.sigmoid(mask_logits)
    stacked = jnp.stack([mask_cells, target, weight])
    padded = padded_2(stacked, (("row", 1), ("col", 2)), HALO)
    core_width = mask_logits.shape[0]
    tile_count = mask_logits.shape[1] // core_width
    pad_width = core_width + 2 * HALO
    wave_re, wave_im = dft_rows(BAND, pad_width)
    whole_bank = lax.all_gather(kernels, ("row", "col"), axis=1, tiled=True)
    tile_grads = [jnp.zeros((core_width, core_width), jnp.float32)]
    loss_global = jnp.float32(0.0)
    for condition in range(CONDITIONS):
        flat_bank = whole_bank[condition]
        spectra = flat_bank.reshape(2, KERNELS, BAND, BAND)
        condition_loss = jnp.float32(0.0)
        part_grad, part_loss = tile_terms(
            padded, spectra[0], spectra[1], wave_re, wave_im, DOSES[condition], HALO
        )
        tile_grads[0] = tile_grads[0] + part_grad
        condition_loss = part_loss
        loss_global = loss_global + lax.psum(condition_loss, ("row", "col"))
    grad_cells = tile_grads[0] * mask_cells * (1.0 - mask_cells)
    square_local = jnp.sum(grad_cells * grad_cells)
    square_global = lax.psum(square_local, ("row", "col"))
    cell_count = lax.axis_size("row") * core_width * lax.axis_size("col") * core_width * tile_count
    loss_value = loss_global / cell_count
    norm_value = jnp.sqrt(square_global / cell_count + EPSILON)
    return (mask_logits - STEP * grad_cells / norm_value, loss_value)


def solution(mesh):
    placed = (P("row", "col"), P("row", "col"), P("row", "col"), P(None, ("row", "col")))
    return jax.shard_map(
        shards, mesh=mesh, in_specs=placed, out_specs=(P("row", "col"), P()), check_vma=False
    )
```

profile of v0, /device:TPU:25, one launch (start us, length us, event | category | flops | bytes accessed | tf_op | source)
XLA Modules:
  0.0 1498.3 jit_solution(4228233007003579788)
XLA Ops:
  2.4 2.7 collective-permute-start.1
  5.2 4.3 collective-permute-start
  9.5 1274.6 %all-gather = f32[512,24,2]{1,2,0:T(2,128)S(1)} all-gather(f32[1,24,2]{1,2,0:T(2,128)} %bitcast.232), channel_id=1, replica_groups=mesh['row'=32,'col'=16] {'row','col'}, dimensions={0}, use_global_device_ids=true | all-gather | bytes 98496 | tf_op jit(solution)/shard_map/all_gather | solution.py:102
  1285.4 1.3 collective-permute-start.3
  1286.7 4.3 collective-permute-start.2
  1291.8 2.2 collective-permute-done.3
  1294.0 1.5 collective-permute-done.2
  1301.6 1.6 fusion.70
  1303.2 2.5 fusion.68
  1305.7 1.6 copy.29
  1307.3 2.1 fusion.132
  1309.4 2.1 fusion.139
  1311.5 1.6 copy.28
  1313.1 1.4 fusion.138
  1314.5 1.4 fusion.130
  1315.9 2.5 fusion.64
  1318.4 1.6 fusion.62
  1320.0 1.8 convolution_subtract_fusion.1
  1321.9 1.7 add_reduce_fusion.1
  1323.6 1.6 convolution_subtract_fusion
  1325.2 1.7 add_reduce_fusion
  1333.1 1.5 fusion
  1334.6 1.3 fusion.31
  1347.6 147.6 %all-reduce = (f32[]{:T(128)}, f32[]{:T(128)}) all-reduce(f32[]{:T(128)} %get-tuple-element.34, f32[]{:T(128)S(6)} %add.285), channel_id=1, replica_groups=mesh['row'=32,'col'=16] {'row','col'}, use_global_device_ids=true, to_apply=%region_7.8 | all-reduce | flops 2 | bytes 16 | tf_op jit(solution)/shard_map/psum | solution.py:117
  (96 shorter events, 26.7 us)
Async XLA Ops:
  2.4 1282.7 %copy-start.13 = (f32[128,128]{1,0:T(8,128)S(1)}, f32[128,128]{1,0:T(8,128)}, u32[]{:S(2)}) copy-start(f32[128,128]{1,0:T(8,128)} %param.6) | copy-start | bytes 196612
  2.4 1282.7 %copy-start.14 = (f32[128,128]{1,0:T(8,128)S(1)}, f32[128,128]{1,0:T(8,128)}, u32[]{:S(2)}) copy-start(f32[128,128]{1,0:T(8,128)} %param.5) | copy-start | bytes 196612
  2.4 1282.7 %collective-permute-start.1 = (f32[3,64,128]{2,1,0:T(8,128)S(1)}, f32[3,64,128]{2,1,0:T(8,128)S(1)}, u32[]{:S(2)}, u32[]{:S(2)}) collective-permute-start(f32[3,64,128]{2,1,0:T(8,128)S(1)} %get-tuple-element.25), channel_id=1, source_target_pairs={{16,0},{32,16},{48,32},{64,48},{80,64},{96,80},{112,96},{128,112},... | collective-permute-start | bytes 294920 | tf_op jit(solution)/shard_map/ppermute | solution.py:26
  5.2 1279.9 %collective-permute-start = (f32[3,64,128]{2,1,0:T(8,128)S(1)}, f32[3,64,128]{2,1,0:T(8,128)S(1)}, u32[]{:S(2)}, u32[]{:S(2)}) collective-permute-start(f32[3,64,128]{2,1,0:T(8,128)S(1)} %get-tuple-element.24), channel_id=1, source_target_pairs={{0,16},{16,32},{32,48},{48,64},{64,80},{80,96},{96,112},{112,128},... | collective-permute-start | bytes 294920 | tf_op jit(solution)/shard_map/ppermute | solution.py:23
  1284.8 13.8 copy-start.9
  1284.9 13.7 copy-start.11
  1285.0 13.7 copy-start.5
  1285.1 13.6 copy-start.7
  1285.4 8.6 collective-permute-start.3
  1286.7 8.8 collective-permute-start.2
  1295.9 0.9 copy-start
  1300.0 1.6 copy-start.4
  1313.1 5.4 copy-start.3
  1321.8 1.7 copy-start.2
  1325.1 1.7 copy-start.1
  1337.1 1.8 copy-start.10
  1337.1 1.8 copy-start.12
  1337.1 2.3 copy-start.17
  1337.1 2.8 copy-start.15
  1339.4 3.1 copy-start.6
  1339.4 3.1 copy-start.8
  1340.7 5.9 copy-start.16
where the time goes:
time: 1500 us
  blocking collectives  1420 us (95%)
  matrix products  44.1 us (3%)
    all_gather x1, blocking collectives, shards(): whole_bank = lax.all_gather(kernels, ('row', 'col'), axis=1, tiled=True)  1270 us
    psum x1, blocking collectives, shards(): square_global = lax.psum(square_local, ('row', 'col'))  148 us
    dot_general x42, matrix products, matmul(): jnp.matmul(first, second, precision=lax.Precision.HIGHEST, preferred_elem...  35.1 us
  transfers between devices with their start and end apart: 4, of which 2 were waited for; matrix products, arithmetic and copies ran while one was open for 0% of the time, Pallas kernels for 0%

commit v1 on v0

--- a/solution.py
+++ b/solution.py
@@ -99,7 +99,10 @@
     tile_count = mask_logits.shape[1] // core_width
     pad_width = core_width + 2 * HALO
     wave_re, wave_im = dft_rows(BAND, pad_width)
-    whole_bank = lax.all_gather(kernels, ("row", "col"), axis=1, tiled=True)
+    whole_bank = jnp.concatenate(
+        lax.all_to_all(jnp.stack([kernels] * lax.axis_size(("row", "col"))), ("row", "col"), 0, 0),
+        axis=1,
+    )
     tile_grads = [jnp.zeros((core_width, core_width), jnp.float32)]
     loss_global = jnp.float32(0.0)
     for condition in range(CONDITIONS):

time: 1500 us -> 215 us (0.14)
  the two profiles are of different devices: /device:TPU:25 before, /device:TPU:1 now
where the time goes in v1:
time: 215 us; the launch traced here: 212 us
  blocking collectives  107 us (50%)
  matrix products  44 us (20%)
  starting transfers between devices  36 us (17%)
  waiting for transfers between devices  7.96 us (4%)
  local copies, waits for them, and re-layouts  7.71 us (4%)
  between operations  5.42 us (3%)
  other arithmetic  3.75 us (2%)
    psum x1, blocking collectives, shards(): square_global = lax.psum(square_local, ('row', 'col'))  107 us
    dot_general x42, matrix products, matmul(): jnp.matmul(first, second, precision=lax.Precision.HIGHEST, preferred_elem...  35 us
    all_to_all x1, starting transfers between devices, shards(): lax.all_to_all(jnp.stack([kernels] * lax.axis_size(('row', 'col'))), ('ro...  22.1 us
    unnamed x8, matrix products  8.98 us
    ppermute x2, starting transfers between devices, padded_2(): lax.ppermute(lax.slice_in_dim(block, 0, width, axis=dim), axis, backward)  7.5 us
    ppermute x2, starting transfers between devices, padded_2(): lax.ppermute(lax.slice_in_dim(block, block.shape[dim] - width, None, axis...  6.4 us
    all_to_all x1, waiting for transfers between devices, shards(): lax.all_to_all(jnp.stack([kernels] * lax.axis_size(('row', 'col'))), ('ro...  4.57 us
  transfers between devices with their start and end apart: 5, of which 3 were waited for; matrix products, arithmetic and copies ran while one was open for 1% of the time, Pallas kernels for 0%

profile of v1, /device:TPU:1, one launch (start us, length us, event | category | flops | bytes accessed | tf_op | source)
XLA Modules:
  0.0 211.5 jit_solution(749131677239985216)
XLA Ops:
  0.7 1.6 stack.10
  2.3 22.1 %all-to-all-start = ((f32[512,2,24]{2,1,0:T(2,128)}), f32[512,2,24]{2,1,0:T(2,128)S(1)}, u32[]{:S(2)}, u32[]{:S(2)}) async-start(f32[512,2,24]{2,1,0:T(2,128)} %stack.10), calls=%async_computation | async-start | bytes 1048576 | tf_op jit(solution)/shard_map/all_to_all | solution.py:103
  24.6 6.2 %collective-permute-start.1 = (f32[3,64,128]{2,1,0:T(8,128)S(1)}, f32[3,64,128]{2,1,0:T(8,128)S(1)}, u32[]{:S(2)}, u32[]{:S(2)}) collective-permute-start(f32[3,64,128]{2,1,0:T(8,128)S(1)} %get-tuple-element.25), channel_id=1, source_target_pairs={{16,0},{32,16},{48,32},{64,48},{80,64},{96,80},{112,96},{128,112},... | collective-permute-start | bytes 294920 | tf_op jit(solution)/shard_map/ppermute | solution.py:26
  30.8 1.9 collective-permute-start
  32.7 3.0 %collective-permute-done.1 = f32[3,64,128]{2,1,0:T(8,128)S(1)} collective-permute-done((f32[3,64,128]{2,1,0:T(8,128)S(1)}, f32[3,64,128]{2,1,0:T(8,128)S(1)}, u32[]{:S(2)}, u32[]{:S(2)}) %collective-permute-start.1) | collective-permute-done | bytes 98336 | tf_op jit(solution)/shard_map/ppermute | solution.py:26
  36.0 1.3 collective-permute-start.3
  37.3 4.5 %collective-permute-start.2 = (f32[3,256,64]{2,1,0:T(8,128)S(1)}, f32[3,256,64]{2,1,0:T(8,128)S(1)}, u32[]{:S(2)}, u32[]{:S(2)}) collective-permute-start(f32[3,256,64]{2,1,0:T(8,128)S(1)} %get-tuple-element.18), channel_id=1, source_target_pairs={{0,1},{1,2},{2,3},{3,4},{4,5},{5,6},{6,7},{7,8},{8,9},{9,10},{10,1... | collective-permute-start | bytes 589832 | tf_op jit(solution)/shard_map/ppermute | solution.py:23
  42.6 4.6 %all-to-all-done = f32[512,2,24]{2,1,0:T(2,128)S(1)} async-done(((f32[512,2,24]{2,1,0:T(2,128)}), f32[512,2,24]{2,1,0:T(2,128)S(1)}, u32[]{:S(2)}, u32[]{:S(2)}) %all-to-all-start) | async-done | bytes 98336 | tf_op jit(solution)/shard_map/all_to_all | solution.py:103
  47.2 1.5 slice_reduce_fusion.1
  55.7 1.6 fusion.70
  57.2 2.5 %fusion.68 = f32[6,256,256]{2,1,0:T(8,128)S(1)} fusion(f32[256,6,32]{0,2,1:T(8,128)S(1)} %bitcast.210, f32[256,6,32]{0,2,1:T(8,128)} %bitcast.208, s32[32]{0:T(128)S(1)} %iota_add_fusion), kind=kOutput, calls=%fused_computation.84 | convolution fusion | flops 151183360 | bytes 1966208 | tf_op jit(solution)/shard_map/dot_general | solution.py:32
  59.7 1.6 copy.27
  61.4 2.1 fusion.132
  63.4 2.1 fusion.139
  65.5 1.6 copy.26
  67.1 1.4 fusion.138
  68.6 1.4 fusion.130
  70.0 2.7 %fusion.64 = f32[6,256,256]{2,1,0:T(8,128)S(1)} fusion(f32[256,6,32]{0,2,1:T(8,128)S(1)} %bitcast.211, f32[256,6,32]{0,2,1:T(8,128)} %bitcast.205, s32[32]{0:T(128)S(1)} %iota_add_fusion), kind=kOutput, calls=%fused_computation.80 | convolution fusion | flops 151166976 | bytes 1966208 | tf_op jit(solution)/shard_map/dot_general | solution.py:32
  72.7 1.6 fusion.62
  74.2 1.6 convolution_subtract_fusion.1
  75.8 1.7 add_reduce_fusion.1
  77.5 1.6 convolution_subtract_fusion
  79.1 1.7 add_reduce_fusion
  101.5 106.7 %all-reduce = (f32[]{:T(128)}, f32[]{:T(128)}) all-reduce(f32[]{:T(128)} %get-tuple-element.34, f32[]{:T(128)S(6)} %add.285), channel_id=1, replica_groups=mesh['row'=32,'col'=16] {'row','col'}, use_global_device_ids=true, to_apply=%region_7.8 | all-reduce | flops 2 | bytes 16 | tf_op jit(solution)/shard_map/psum | solution.py:120
  (98 shorter events, 27.6 us)
Async XLA Ops:
  0.6 23.8 %copy-start.16 = (f32[128,128]{1,0:T(8,128)S(1)}, f32[128,128]{1,0:T(8,128)}, u32[]{:S(2)}) copy-start(f32[128,128]{1,0:T(8,128)} %param.4) | copy-start | bytes 196612
  0.6 23.9 %copy-start.13 = (f32[128,128]{1,0:T(8,128)S(1)}, f32[128,128]{1,0:T(8,128)}, u32[]{:S(2)}) copy-start(f32[128,128]{1,0:T(8,128)} %param.6) | copy-start | bytes 196612
  0.7 23.9 %copy-start.14 = (f32[128,128]{1,0:T(8,128)S(1)}, f32[128,128]{1,0:T(8,128)}, u32[]{:S(2)}) copy-start(f32[128,128]{1,0:T(8,128)} %param.5) | copy-start | bytes 196612
  2.3 44.8 %all-to-all-start = ((f32[512,2,24]{2,1,0:T(2,128)}), f32[512,2,24]{2,1,0:T(2,128)S(1)}, u32[]{:S(2)}, u32[]{:S(2)}) async-start(f32[512,2,24]{2,1,0:T(2,128)} %stack.10), calls=%async_computation | async-start | bytes 1048576 | tf_op jit(solution)/shard_map/all_to_all | solution.py:103
  24.6 11.2 %collective-permute-start.1 = (f32[3,64,128]{2,1,0:T(8,128)S(1)}, f32[3,64,128]{2,1,0:T(8,128)S(1)}, u32[]{:S(2)}, u32[]{:S(2)}) collective-permute-start(f32[3,64,128]{2,1,0:T(8,128)S(1)} %get-tuple-element.25), channel_id=1, source_target_pairs={{16,0},{32,16},{48,32},{64,48},{80,64},{96,80},{112,96},{128,112},... | collective-permute-start | bytes 294920 | tf_op jit(solution)/shard_map/ppermute | solution.py:26
  30.8 5.0 %collective-permute-start = (f32[3,64,128]{2,1,0:T(8,128)S(1)}, f32[3,64,128]{2,1,0:T(8,128)S(1)}, u32[]{:S(2)}, u32[]{:S(2)}) collective-permute-start(f32[3,64,128]{2,1,0:T(8,128)S(1)} %get-tuple-element.24), channel_id=1, source_target_pairs={{0,16},{16,32},{32,48},{48,64},{64,80},{80,96},{96,112},{112,128},... | collective-permute-start | bytes 294920 | tf_op jit(solution)/shard_map/ppermute | solution.py:23
  36.0 13.2 %collective-permute-start.3 = (f32[3,256,64]{2,1,0:T(8,128)S(1)}, f32[3,256,64]{2,1,0:T(8,128)S(1)}, u32[]{:S(2)}, u32[]{:S(2)}) collective-permute-start(f32[3,256,64]{2,1,0:T(8,128)S(1)} %get-tuple-element.19), channel_id=1, source_target_pairs={{1,0},{2,1},{3,2},{4,3},{5,4},{6,5},{7,6},{8,7},{9,8},{10,9},{11,1... | collective-permute-start | bytes 589832 | tf_op jit(solution)/shard_map/ppermute | solution.py:26
  37.3 12.2 %collective-permute-start.2 = (f32[3,256,64]{2,1,0:T(8,128)S(1)}, f32[3,256,64]{2,1,0:T(8,128)S(1)}, u32[]{:S(2)}, u32[]{:S(2)}) collective-permute-start(f32[3,256,64]{2,1,0:T(8,128)S(1)} %get-tuple-element.18), channel_id=1, source_target_pairs={{0,1},{1,2},{2,3},{3,4},{4,5},{5,6},{6,7},{7,8},{8,9},{9,10},{10,1... | collective-permute-start | bytes 589832 | tf_op jit(solution)/shard_map/ppermute | solution.py:23
  48.7 3.9 %copy-start.9 = (f32[6,32,32]{2,1,0:T(8,128)}, f32[6,32,32]{2,1,0:T(8,128)S(1)}, u32[]{:S(2)}) copy-start(f32[6,32,32]{2,1,0:T(8,128)S(1)} %squeeze.26) | copy-start | bytes 73732
  48.9 3.8 %copy-start.11 = (f32[6,32,32]{2,1,0:T(8,128)}, f32[6,32,32]{2,1,0:T(8,128)S(1)}, u32[]{:S(2)}) copy-start(f32[6,32,32]{2,1,0:T(8,128)S(1)} %squeeze.24) | copy-start | bytes 73732
  49.0 3.7 %copy-start.5 = (f32[6,32,32]{2,1,0:T(8,128)}, f32[6,32,32]{2,1,0:T(8,128)S(1)}, u32[]{:S(2)}) copy-start(f32[6,32,32]{2,1,0:T(8,128)S(1)} %squeeze.27) | copy-start | bytes 73732
  49.1 3.6 %copy-start.7 = (f32[6,32,32]{2,1,0:T(8,128)}, f32[6,32,32]{2,1,0:T(8,128)S(1)}, u32[]{:S(2)}) copy-start(f32[6,32,32]{2,1,0:T(8,128)S(1)} %squeeze.28) | copy-start | bytes 73732
  49.9 0.9 copy-start
  54.0 1.6 copy-start.4
  67.1 5.5 %copy-start.3 = (f32[256,192]{0,1:S(1)}, f32[256,192]{0,1}, u32[]{:S(2)}) copy-start(f32[256,192]{0,1} %fusion.132) | copy-start | bytes 589828
  75.8 1.7 copy-start.2
  79.1 1.7 copy-start.1
  91.0 1.8 copy-start.10
  91.0 1.8 copy-start.12
  91.0 2.3 %copy-start.18 = (f32[32,256]{1,0:T(8,128)S(1)}, f32[32,256]{1,0:T(8,128)}, u32[]{:S(2)}) copy-start(f32[32,256]{1,0:T(8,128)} %get-tuple-element.29) | copy-start | bytes 98308
  91.0 2.8 %copy-start.15 = (f32[32,256]{1,0:T(8,128)S(1)}, f32[32,256]{1,0:T(8,128)}, u32[]{:S(2)}) copy-start(f32[32,256]{1,0:T(8,128)} %get-tuple-element.28) | copy-start | bytes 98308
  93.3 3.1 %copy-start.6 = (f32[6,32,32]{2,1,0:T(8,128)S(1)}, f32[6,32,32]{2,1,0:T(8,128)}, u32[]{:S(2)}) copy-start(f32[6,32,32]{2,1,0:T(8,128)} %copy-done.5) | copy-start | bytes 73732
  93.4 3.1 %copy-start.8 = (f32[6,32,32]{2,1,0:T(8,128)S(1)}, f32[6,32,32]{2,1,0:T(8,128)}, u32[]{:S(2)}) copy-start(f32[6,32,32]{2,1,0:T(8,128)} %copy-done.7) | copy-start | bytes 73732
  94.6 5.9 %copy-start.17 = (f32[128,128]{1,0:T(8,128)S(1)}, f32[128,128]{1,0:T(8,128)}, u32[]{:S(2)}) copy-start(f32[128,128]{1,0:T(8,128)} %param.4) | copy-start | bytes 196612
